TPU v7x, 128 devices: a whole 4x4x4 slice. The times are simulated.
128 devices in a mesh: tok: 4 (over y), seq: 16 (over z, x), kv: 2 (over core).
Axes of the slice: x: 4, y: 4, z: 4, core: 2. Of those that a mesh axis runs over, the one named last changes fastest.
Arguments:
- token_ids: int32 [64, 4], replicated, may hold values from 0 to 32767
- request_order: int32 [64], replicated, may hold values from 0 to 63, each once
- cache_lengths: int32 [64], replicated, may hold values from 1 to 16384, 524288 in all
- embed_table: bfloat16 [32768, 2048], P(('tok', 'kv'), 'seq'), may hold values from -3 to 3
- attn_gain: bfloat16 [2048], replicated, may hold values from 0.099609375 to 1.8984375
- proj_query: bfloat16 [2048, 2048], P(None, ('tok', 'kv')), may hold values from -0.125 to 0.125
- proj_kv: bfloat16 [2048, 8, 128], P(None, ('tok', 'kv')), may hold values from -0.125 to 0.125
- kv_cache: bfloat16 [64, 16384, 8, 128], P(None, 'seq', ('tok', 'kv')), may hold values from -125 to 125, as said below
- proj_out: bfloat16 [2048, 2048], P(('tok', 'kv'), 'seq'), may hold values from -0.25 to 0.25
- mlp_gain: bfloat16 [2048], replicated, may hold values from 0.099609375 to 1.8984375
- proj_gate: bfloat16 [2048, 8192], P(None, 'seq'), may hold values from -0.125 to 0.125
- proj_up: bfloat16 [2048, 8192], P(None, 'seq'), may hold values from -0.125 to 0.125
- proj_down: bfloat16 [8192, 2048], P('seq'), may hold values from -0.0625 to 0.0625
Outputs:
- hidden_out: bfloat16 [64, 4, 2048], P(('tok', 'kv'), None, 'seq')
Inputs may be any that keep to these rules, and one draw needn't show every extreme that they name: `request_order`: every request stands in exactly one slot. `cache_lengths`: the lengths sum to 524288 and the largest equals 16384. `kv_cache`: cached keys are already rotated to their positions.
All inputs are finite; a program needn't handle non-finite values.
Results may differ from a plain program's by a relative error of at most 0.018.
The roundings to bfloat16 on the way count: a program that leaves them out, or rounds other values in their place, can miss the bound.
Values may be sent and summed in bfloat16 or wider, within the bound.
A program may use at most 128 MiB of HBM per device.

v0:
```python
import jax
import jax.numpy as jnp
from jax import lax
from jax.sharding import PartitionSpec as P

EPSILON = 1e-05
ROPE_BASE = 1000000.0
FLOOR_SCORE = -1e30


def combined_all(value, axis, join):
    pieces = jax.tree.map(lambda part: lax.all_gather(part, axis), value)
    head = jax.tree.map(lambda part: part[0], pieces)
    tail = jax.tree.map(lambda part: part[1:], pieces)
    so_far, _ = lax.scan(lambda so_far, share: (join(so_far, share), None), head, tail)
    return so_far


def rotate(vector, position):
    half_dim = vector.shape[-1] // 2
    frequency = ROPE_BASE ** (-(jnp.arange(half_dim, dtype=jnp.float32) * 2.0 / vector.shape[-1]))
    angles = position[..., None] * frequency
    cosine = jnp.cos(angles)
    sine_part = jnp.sin(angles)
    front_half = vector[..., :half_dim]
    back_half = vector[..., half_dim:]
    return jnp.concatenate(
        [front_half * cosine - back_half * sine_part, back_half * cosine + front_half * sine_part],
        axis=-1,
    )


def combine(earlier, later):
    peak_a, mass_a, accum_a = earlier
    peak_b, mass_b, accum_b = later
    highest = jnp.maximum(peak_a, peak_b)
    factor_a = jnp.exp(peak_a - highest)
    factor_b = jnp.exp(peak_b - highest)
    return (
        highest,
        mass_a * factor_a + mass_b * factor_b,
        accum_a * factor_a[..., None] + accum_b * factor_b[..., None],
    )


def per_device(
    token_ids,
    request_order,
    cache_lengths,
    embed_table,
    attn_gain,
    proj_query,
    proj_kv,
    kv_cache,
    proj_out,
    mlp_gain,
    proj_gate,
    proj_up,
    proj_down,
):
    n_req, n_steps = token_ids.shape
    width = proj_query.shape[0]
    head_dim = kv_cache.shape[-1] // 2
    group_heads = proj_query.shape[1] // head_dim
    ctx_dev = kv_cache.shape[1]
    columns = embed_table.shape[1]
    vocab_rows = embed_table.shape[0]
    scale = head_dim ** (-0.5)
    owners = lax.axis_size("tok") * lax.axis_size("kv")
    owner_index = lax.axis_index("tok") * lax.axis_size("kv") + lax.axis_index("kv")
    seq_rank = lax.axis_index("seq")
    offset = token_ids.reshape(-1) - owner_index * vocab_rows
    inside = (offset >= 0) & (offset < vocab_rows)
    picked = jnp.take(embed_table, jnp.clip(offset, 0, vocab_rows - 1), axis=0)
    partial_x = jnp.where(inside[:, None], picked.astype(jnp.float32), 0.0)
    local_x = lax.psum(partial_x.astype(jnp.bfloat16), ("tok", "kv"))
    kv_flat = proj_kv.reshape(width, -1)
    full_x = lax.all_gather(local_x, "seq", axis=1, tiled=True)
    widened = full_x.astype(jnp.float32)
    square_mean = jnp.mean(widened * widened, axis=1)
    scaled = (widened * attn_gain.astype(jnp.float32)).astype(jnp.bfloat16)
    q_raw = jnp.dot(scaled, proj_query, preferred_element_type=jnp.float32)
    kv_raw = jnp.dot(scaled, kv_flat, preferred_element_type=jnp.float32)
    inv_norm = lax.rsqrt(square_mean + EPSILON)[:, None]
    q_scaled = (q_raw * inv_norm).reshape(n_req, n_steps, group_heads, head_dim)
    kv_scaled = (kv_raw * inv_norm).reshape(n_req, n_steps, 2 * head_dim)
    position = (cache_lengths[:, None] + jnp.arange(n_steps, dtype=jnp.int32)[None, :]).astype(
        jnp.float32
    )
    query = rotate(q_scaled, position[:, :, None]).astype(jnp.bfloat16)
    new_keys = rotate(kv_scaled[..., :head_dim], position).astype(jnp.bfloat16)
    new_values = kv_scaled[..., head_dim:].astype(jnp.bfloat16)
    cache_rows = kv_cache[:, :, 0, :]
    key_part = cache_rows[..., :head_dim]
    value_part = cache_rows[..., head_dim:]
    scores = (
        jnp.einsum("rjgd,rpd->rjgp", query, key_part, preferred_element_type=jnp.float32) * scale
    )
    places = seq_rank * ctx_dev + jnp.arange(ctx_dev, dtype=jnp.int32)
    is_live = (places[None, :] < cache_lengths[:, None])[:, None, None, :]
    masked = jnp.where(is_live, scores, FLOOR_SCORE)
    block_peak = jnp.max(masked, axis=-1)
    block_weight = jnp.where(is_live, jnp.exp(masked - block_peak[..., None]), 0.0).astype(
        jnp.bfloat16
    )
    block_mass = jnp.sum(block_weight.astype(jnp.float32), axis=-1)
    block_accum = jnp.einsum(
        "rjgp,rpd->rjgd", block_weight, value_part, preferred_element_type=jnp.float32
    )
    peak_all, mass_all, accum_all = combined_all(
        (block_peak, block_mass, block_accum), "seq", combine
    )
    fresh_scores = (
        jnp.einsum("rjgd,rkd->rjgk", query, new_keys, preferred_element_type=jnp.float32) * scale
    )
    causal = (jnp.arange(n_steps)[:, None] >= jnp.arange(n_steps)[None, :])[None, :, None, :]
    fresh_masked = jnp.where(causal, fresh_scores, FLOOR_SCORE)
    fresh_peak = jnp.max(fresh_masked, axis=-1)
    fresh_weight = jnp.where(causal, jnp.exp(fresh_masked - fresh_peak[..., None]), 0.0).astype(
        jnp.bfloat16
    )
    fresh_mass = jnp.sum(fresh_weight.astype(jnp.float32), axis=-1)
    fresh_accum = jnp.einsum(
        "rjgk,rkd->rjgd", fresh_weight, new_values, preferred_element_type=jnp.float32
    )
    highest = jnp.maximum(peak_all, fresh_peak)
    cache_factor = jnp.exp(peak_all - highest)
    fresh_factor = jnp.exp(fresh_peak - highest)
    numer = accum_all * cache_factor[..., None] + fresh_accum * fresh_factor[..., None]
    denom = mass_all * cache_factor + fresh_mass * fresh_factor
    attended = (
        (numer / denom[..., None])
        .astype(jnp.bfloat16)
        .reshape(n_req, n_steps, group_heads * head_dim)
    )
    slot_rows = attended[request_order].reshape(n_req * n_steps, group_heads * head_dim)
    per_owner = n_req // owners
    attn_part = lax.psum_scatter(
        jnp.dot(slot_rows, proj_out, preferred_element_type=jnp.float32),
        ("tok", "kv"),
        scatter_dimension=0,
        tiled=True,
    )
    my_requests = lax.dynamic_slice_in_dim(request_order, owner_index * per_owner, per_owner)
    own_x = local_x.reshape(n_req, n_steps, columns)[my_requests].reshape(
        per_owner * n_steps, columns
    )
    mid = (own_x.astype(jnp.float32) + attn_part).astype(jnp.bfloat16)
    piece_wide = lax.all_gather(mid, "seq", axis=1, tiled=True).astype(jnp.float32)
    gain_part = mlp_gain.astype(jnp.float32)
    piece_scaled = (piece_wide * gain_part).astype(jnp.bfloat16)
    gate_acc = jnp.dot(piece_scaled, proj_gate, preferred_element_type=jnp.float32)
    up_acc = jnp.dot(piece_scaled, proj_up, preferred_element_type=jnp.float32)
    square_total = jnp.sum(piece_wide * piece_wide, axis=1)
    inv_mlp = lax.rsqrt(square_total / width + EPSILON)[:, None]
    hidden = (jax.nn.silu(gate_acc * inv_mlp) * (up_acc * inv_mlp)).astype(jnp.bfloat16)
    down_terms = jnp.dot(hidden, proj_down, preferred_element_type=jnp.float32)
    mlp_part = lax.psum_scatter(down_terms, "seq", scatter_dimension=1, tiled=True)
    result = (mid.astype(jnp.float32) + mlp_part).astype(jnp.bfloat16)
    return result.reshape(per_owner, n_steps, columns)


def solution(mesh):
    placed = (
        P(),
        P(),
        P(),
        P(("tok", "kv"), "seq"),
        P(),
        P(None, ("tok", "kv")),
        P(None, ("tok", "kv"), None),
        P(None, "seq", ("tok", "kv"), None),
        P(("tok", "kv"), "seq"),
        P(),
        P(None, "seq"),
        P(None, "seq"),
        P("seq", None),
    )
    return jax.shard_map(
        per_device,
        mesh=mesh,
        in_specs=placed,
        out_specs=P(("tok", "kv"), None, "seq"),
        check_vma=False,
    )
```

profile of v0, /device:TPU:0, one launch (start us, length us, event | category | flops | bytes accessed | tf_op | source)
XLA Modules:
  0.0 429.6 jit_solution(7146980658867892863)
XLA Ops:
  11.6 61.3 %all-reduce.2.cloned.1.call-done = bf16[256,128]{1,0:T(8,128)(2,1)} async-done(((bf16[256,128]{1,0:T(8,128)(2,1)}), bf16[256,128]{1,0:T(8,128)(2,1)}) %all-reduce.2.cloned.1.call-update) | async-done | bytes 65552 | tf_op jit(solution)/shard_map/psum | solution.py:76
  73.6 22.1 %copy.87 = bf16[64,1024,1,128]{1,3,0,2:T(8,128)(2,1)} copy(bf16[64,1024,1,128]{3,1,2,0:T(8,128)(2,1)} %param.22) | data formatting | bytes 33554432 | tf_op args[7]
  96.5 21.2 %all-gather.6.cloned.1.call-done = bf16[256,2048]{1,0:T(8,128)(2,1)} async-done(((bf16[256,128]{1,0:T(8,128)(2,1)}), bf16[256,2048]{1,0:T(8,128)(2,1)}) %all-gather.6.cloned.1.call-update) | async-done | bytes 1048592 | tf_op jit(solution)/shard_map/all_gather | solution.py:78
  125.2 6.2 %fusion.5 = (f32[64,4,4]{2,1,0:T(4,128)S(1)}, f32[64,4,4,1024]{3,2,1,0:T(4,128)S(1)}) fusion(pred[64,1024]{1,0:T(8,128)(4,1)} %broadcast_compare_fusion, bf16[64,1024,128]{1,2,0:T(8,128)(2,1)} %bitcast.67, bf16[64,4,4,32]{3,2,1,0:T(4,128)(2,1)S(1)} %get-tuple-element.101, bf16[64,4,4,32]{3,2,1,0:T(4,128)(2,1)S(1)} %get-tuple-element.100), kind=kOutput, calls=%fused_computation.18 | convolution fusion | flops 137624576 | bytes 12783616 | tf_op jit(solution)/shard_map/rjgd,rpd->rjgp/dot_general | solution.py:97
  131.4 3.7 convert_reduce_fusion
  135.1 6.8 %fusion.3 = f32[64,4,4,64]{3,2,1,0:T(4,128)} fusion(bf16[64,4,4,1024]{3,2,1,0:T(4,128)(2,1)S(1)} %get-tuple-element.99, bf16[64,1024,128]{1,2,0:T(8,128)(2,1)} %bitcast.68), kind=kOutput, calls=%fused_computation.12 | convolution fusion | flops 134217728 | bytes 10747904 | tf_op jit(solution)/shard_map/rjgp,rpd->rjgd/dot_general | solution.py:107
  142.7 30.8 %all-gather.1 = f32[1024,4,4]{2,1,0:T(4,128)S(1)} all-gather(f32[64,4,4]{2,1,0:T(4,128)S(1)} %get-tuple-element.98), channel_id=3, replica_groups=mesh['tok'=4,'seq'=16,'kv'=2] {'seq'}, dimensions={0}, use_global_device_ids=true | all-gather | bytes 69632 | tf_op jit(solution)/shard_map/all_gather | solution.py:12
  174.9 32.0 %all-gather = f32[1024,4,4]{2,1,0:T(4,128)S(1)} all-gather(f32[64,4,4]{2,1,0:T(4,128)S(1)} %get-tuple-element.110), channel_id=2, replica_groups=mesh['tok'=4,'seq'=16,'kv'=2] {'seq'}, dimensions={0}, use_global_device_ids=true | all-gather | bytes 69632 | tf_op jit(solution)/shard_map/all_gather | solution.py:12
  209.1 3.3 fusion.36
  214.6 2.7 copy.93
  219.6 5.8 %all-gather.8.cloned.1.call-done = f32[1024,4,4,64]{3,2,1,0:T(4,128)} async-done(((f32[64,4,4,64]{3,2,1,0:T(4,128)}), f32[1024,4,4,64]{3,2,1,0:T(4,128)}) %all-gather.8.cloned.1.call-update) | async-done | bytes 4194320 | tf_op jit(solution)/shard_map/all_gather | solution.py:12
  225.3 7.7 %slice.77 = f32[960,4,4,64]{3,2,1,0:T(4,128)} slice(f32[1024,4,4,64]{3,2,1,0:T(4,128)} %all-gather.8.cloned.1.call-done), slice={[64:1024], [0:4], [0:4], [0:64]} | slice | bytes 7864320 | tf_op jit(solution)/shard_map/slice | solution.py:14
  233.1 53.9 %while.14 = (s32[]{:T(128)}, f32[64,4,4]{0,2,1:T(4,128)S(1)}, f32[64,4,4]{0,2,1:T(4,128)S(1)}, f32[64,4,4,64]{3,2,1,0:T(4,128)S(1)}, f32[15,64,4,4]{1,3,2,0:T(4,...) while((s32[]{:T(128)}, f32[64,4,4]{0,2,1:T(4,128)S(1)}, ...), condition=%wide.region_5.6_spmd, body=%wide.region_4.5_spmd.sunk | while | flops 202754 | bytes 843877 | solution.py:15
  234.1 2.6 fusion.54
  237.7 2.6 fusion.54
  244.9 2.6 fusion.54
  248.5 2.6 fusion.54
  252.1 2.6 fusion.54
  255.7 2.6 fusion.54
  262.8 2.6 fusion.54
  294.2 28.3 %reduce-scatter.3.cloned.1.call-done = f32[32,128]{1,0:T(8,128)} async-done(((f32[256,128]{1,0:T(8,128)}), f32[32,128]{1,0:T(8,128)}) %reduce-scatter.3.cloned.1.call-update) | async-done | bytes 16400 | tf_op jit(solution)/shard_map/reduce_scatter | solution.py:138
  323.3 23.9 %all_gather.31 = bf16[32,2048]{1,0:T(8,128)(2,1)S(1)} all-gather(bf16[32,128]{1,0:T(8,128)(2,1)S(1)} %fusion.32), channel_id=1, replica_groups=mesh['tok'=4,'seq'=16,'kv'=2] {'seq'}, dimensions={1}, use_global_device_ids=true | all-gather | bytes 139264 | tf_op jit(solution)/shard_map/all_gather | solution.py:149
  349.4 3.2 fusion.13
  352.6 69.2 %reduce-scatter.5.cloned.1.call-done = f32[32,128]{1,0:T(8,128)} async-done(((f32[32,2048]{1,0:T(8,128)}), f32[32,128]{1,0:T(8,128)}) %reduce-scatter.5.cloned.1.call-update) | async-done | bytes 16400 | tf_op jit(solution)/shard_map/reduce_scatter | solution.py:158
  (150 shorter events, 69.7 us)
Async XLA Ops:
  6.5 342.8 %copy-start = (bf16[512,2048]{1,0:T(8,128)(2,1)S(1)}, bf16[512,2048]{1,0:T(8,128)(2,1)}, u32[]{:S(2)}) copy-start(bf16[512,2048]{1,0:T(8,128)(2,1)} %param.27) | copy-start | bytes 6291460
  6.5 66.3 %all-reduce.2.cloned.1.call-start = ((), (), s32[]{:S(2)}) async-start(), calls=%async_computation.2 | async-start | bytes 131072 | tf_op jit(solution)/shard_map/psum | solution.py:76
  11.5 106.1 %all-gather.6.cloned.1.call-start = ((), (), s32[]{:S(2)}) async-start(), calls=%async_computation.3 | async-start | bytes 1114112 | tf_op jit(solution)/shard_map/all_gather | solution.py:78
  72.9 152.4 %all-gather.8.cloned.1.call-start = ((), (), s32[]{:S(2)}) async-start(), calls=%async_computation.6 | async-start | bytes 8912896 | tf_op jit(solution)/shard_map/all_gather | solution.py:12
  73.6 22.1 %copy-start.7 = (s32[64]{0:T(128)S(1)}, s32[64]{0:T(128)}, u32[]{:S(2)}) copy-start(s32[64]{0:T(128)} %param.17) | copy-start | bytes 772
  125.2 6.2 %copy-start.1 = (pred[64,1024]{1,0:T(8,128)(4,1)S(1)}, pred[64,1024]{1,0:T(8,128)(4,1)}, u32[]{:S(2)}) copy-start(pred[64,1024]{1,0:T(8,128)(4,1)} %broadcast_compare_fusion) | copy-start | bytes 196612
  135.1 6.9 %copy-start.9 = (s32[64]{0:T(128)S(1)}, s32[64]{0:T(128)}, u32[]{:S(2)}) copy-start(s32[64]{0:T(128)} %param.16) | copy-start | bytes 772
  142.0 180.5 %reduce-scatter.3.cloned.1.call-start = ((), (), s32[]{:S(2)}) async-start(), calls=%async_computation.4 | async-start | bytes 147456 | tf_op jit(solution)/shard_map/reduce_scatter | solution.py:138
  142.1 70.6 %copy-start.8 = (pred[4,4]{1,0:T(4,128)(4,1)}, pred[4,4]{1,0:T(4,128)(4,1)S(1)}, u32[]{:S(2)}) copy-start(pred[4,4]{1,0:T(4,128)(4,1)S(1)} %iota_compare_fusion) | copy-start | bytes 52
  174.9 33.4 %copy-start.3 = (bf16[64,4,32]{0,2,1:T(8,128)(2,1)S(1)}, bf16[64,4,32]{0,2,1:T(8,128)(2,1)}, u32[]{:S(2)}) copy-start(bf16[64,4,32]{0,2,1:T(8,128)(2,1)} %get-tuple-element.108) | copy-start | bytes 49156
  174.9 33.4 %copy-start.4 = (bf16[64,4,32]{0,2,1:T(8,128)(2,1)S(1)}, bf16[64,4,32]{0,2,1:T(8,128)(2,1)}, u32[]{:S(2)}) copy-start(bf16[64,4,32]{0,2,1:T(8,128)(2,1)} %get-tuple-element.109) | copy-start | bytes 49156
  225.3 7.7 %slice-start = ((f32[1024,4,4,64]{3,2,1,0:T(4,128)}), f32[64,4,4,64]{3,2,1,0:T(4,128)S(1)}, s32[]{:S(2)}) async-start(f32[1024,4,4,64]{3,2,1,0:T(4,128)} %all-gather.8.cloned.1.call-done), calls=%async_computation.7 | async-start | bytes 1048576 | tf_op jit(solution)/shard_map/slice | solution.py:13
  233.1 55.7 %copy-start.2 = (bf16[64,4,4,4]{3,2,1,0:T(4,128)(2,1)S(1)}, bf16[64,4,4,4]{3,2,1,0:T(4,128)(2,1)}, u32[]{:S(2)}) copy-start(bf16[64,4,4,4]{3,2,1,0:T(4,128)(2,1)} %copy.102) | copy-start | bytes 24580
  288.7 3.1 copy-start.5
  288.7 4.0 copy-start.6
  288.7 4.0 copy-start.10
  292.6 129.1 %reduce-scatter.5.cloned.1.call-start = ((), (), s32[]{:S(2)}) async-start(), calls=%async_computation.5 | async-start | bytes 278528 | tf_op jit(solution)/shard_map/reduce_scatter | solution.py:158
Sparse Core Ops, SparseCore 0:
  11.7 61.1 all-reduce.1
  75.2 42.4 all-gather.5
  142.1 83.1 all-gather.7
  292.8 29.7 reduce-scatter.2
  352.7 68.9 reduce-scatter.4
where the time goes:
time: 432 us; the launch traced here: 430 us
  waiting for transfers between devices  186 us (43%)
  blocking collectives  86.6 us (20%)
  other arithmetic  63.8 us (15%)
  local copies, waits for them, and re-layouts  51.2 us (12%)
  matrix products  28.1 us (7%)
  between operations  13.4 us (3%)
    reduce_scatter x1, waiting for transfers between devices, per_device(): lax.psum_scatter(down_terms, 'seq', scatter_dimension=1, tiled=True)  69.2 us
    all_gather x2, blocking collectives, combined_all(): pieces = jax.tree.map(lambda part: lax.all_gather(part, axis), value)  62.8 us
    psum x1, waiting for transfers between devices, per_device(): local_x = lax.psum(partial_x.astype(jnp.bfloat16), ('tok', 'kv'))  61.3 us
    add x15, other arithmetic, combine(): accum_a * factor_a[..., None] + accum_b * factor_b[..., None]  38.7 us
    reduce_scatter x1, waiting for transfers between devices, per_device(): lax.psum_scatter(jnp.dot(slot_rows, proj_out, preferred_element_type=jnp....  28.3 us
    all_gather x1, blocking collectives, per_device(): lax.all_gather(mid, 'seq', axis=1, tiled=True).astype(jnp.float32)  23.9 us
    unnamed x25, local copies, waits for them, and re-layouts  22.3 us
    all_gather x1, waiting for transfers between devices, per_device(): full_x = lax.all_gather(local_x, 'seq', axis=1, tiled=True)  21.2 us
  transfers between devices with their start and end apart: 5, of which 5 were waited for; matrix products, arithmetic and copies ran while one was open for 9% of the time, Pallas kernels for 0%

commit v1 on v0

--- a/solution.py
+++ b/solution.py
@@ -6,6 +6,25 @@
 EPSILON = 1e-05
 ROPE_BASE = 1000000.0
 FLOOR_SCORE = -1e30
+
+
+def core_supply(s0):
+    dev_n = lax.axis_size("seq")
+    pages = list(map(lambda p: (p, (p + 1) % dev_n), range(dev_n)))
+    after = range(dev_n)
+    last = map(lambda p: (p, (p - 1) % dev_n), after)
+    buffer = list(last)
+    raw_out, spare = ([s0], [s0])
+    for _ in range(dev_n // 2):
+        known = lax.ppermute(raw_out[-1], axis_name="seq", perm=pages)
+        raw_out.append(known)
+    for _ in range((dev_n - 1) // 2):
+        a_now = lax.ppermute(spare[-1], axis_name="seq", perm=buffer)
+        spare.append(a_now)
+    big = jnp.concatenate([*raw_out[::-1], *spare[1:]], axis=1)
+    lower = lax.axis_index("seq")
+    step_out = jnp.roll(big, (lower - dev_n // 2) * s0.shape[1], axis=1)
+    return step_out
 
 
 def combined_all(value, axis, join):
@@ -146,7 +165,7 @@
         per_owner * n_steps, columns
     )
     mid = (own_x.astype(jnp.float32) + attn_part).astype(jnp.bfloat16)
-    piece_wide = lax.all_gather(mid, "seq", axis=1, tiled=True).astype(jnp.float32)
+    piece_wide = core_supply(mid).astype(jnp.float32)
     gain_part = mlp_gain.astype(jnp.float32)
     piece_scaled = (piece_wide * gain_part).astype(jnp.bfloat16)
     gate_acc = jnp.dot(piece_scaled, proj_gate, preferred_element_type=jnp.float32)

time: 432 us -> 466 us (1.079)
  starting transfers between devices: 0.17 us -> 39.2 us
  blocking collectives: 86.6 us -> 61.8 us
  waiting for transfers between devices: 186 us -> 204 us
    ppermute x0 -> x15, starting transfers between devices: none -> 39 us  [the longest x7 37.5 us: core_supply(): a_now = lax.ppermute(spare[-1], axis_name='seq', perm=buffer)]
    all_gather x1 -> x0, blocking collectives: 23.9 us -> none  [per_device(): lax.all_gather(mid, 'seq', axis=1, tiled=True).astype(jnp.float32)]
    ppermute x0 -> x15, waiting for transfers between devices: none -> 16.7 us  [the longest x8 16.7 us: core_supply(): known = lax.ppermute(raw_out[-1], axis_name='seq', perm=pages)]
    unnamed x25 -> x54, local copies, waits for them, and re-layouts: 22.3 us -> 22.9 us
  transfers between devices with their start and end apart: 5 -> 20, of which waited for: 5 -> 13; matrix products, arithmetic and copies ran while one was open for 9% -> 9% of each run, Pallas kernels for 0% -> 0%
where the time goes in v1:
time: 466 us; the launch traced here: 464 us
  waiting for transfers between devices  204 us (44%)
  other arithmetic  64.4 us (14%)
  blocking collectives  61.8 us (13%)
  local copies, waits for them, and re-layouts  51.7 us (11%)
  starting transfers between devices  39.2 us (8%)
  matrix products  28.1 us (6%)
  between operations  13.5 us (3%)
    reduce_scatter x1, waiting for transfers between devices, per_device(): lax.psum_scatter(down_terms, 'seq', scatter_dimension=1, tiled=True)  70.8 us
    all_gather x2, blocking collectives, combined_all(): pieces = jax.tree.map(lambda part: lax.all_gather(part, axis), value)  61.8 us
    psum x1, waiting for transfers between devices, per_device(): local_x = lax.psum(partial_x.astype(jnp.bfloat16), ('tok', 'kv'))  61.3 us
    add x15, other arithmetic, combine(): accum_a * factor_a[..., None] + accum_b * factor_b[..., None]  38.7 us
    ppermute x7, starting transfers between devices, core_supply(): a_now = lax.ppermute(spare[-1], axis_name='seq', perm=buffer)  37.5 us
    reduce_scatter x1, waiting for transfers between devices, per_device(): lax.psum_scatter(jnp.dot(slot_rows, proj_out, preferred_element_type=jnp....  27.4 us
    unnamed x54, local copies, waits for them, and re-layouts  22.9 us
    all_gather x1, waiting for transfers between devices, per_device(): full_x = lax.all_gather(local_x, 'seq', axis=1, tiled=True)  20.9 us
  transfers between devices with their start and end apart: 20, of which 13 were waited for; matrix products, arithmetic and copies ran while one was open for 9% of the time, Pallas kernels for 0%

profile of v1, /device:TPU:0, one launch (start us, length us, event | category | flops | bytes accessed | tf_op | source)
XLA Modules:
  0.0 463.6 jit_solution(14796756354406097704)
XLA Ops:
  12.8 61.3 %all-reduce.2.cloned.1.call-done = bf16[256,128]{1,0:T(8,128)(2,1)} async-done(((bf16[256,128]{1,0:T(8,128)(2,1)}), bf16[256,128]{1,0:T(8,128)(2,1)}) %all-reduce.2.cloned.1.call-update) | async-done | bytes 65552 | tf_op jit(solution)/shard_map/psum | solution.py:95
  74.9 22.4 %copy.87 = bf16[64,1024,1,128]{1,3,0,2:T(8,128)(2,1)} copy(bf16[64,1024,1,128]{3,1,2,0:T(8,128)(2,1)} %param.22) | data formatting | bytes 33554432 | tf_op args[7]
  98.0 20.9 %all-gather.6.cloned.1.call-done = bf16[256,2048]{1,0:T(8,128)(2,1)} async-done(((bf16[256,128]{1,0:T(8,128)(2,1)}), bf16[256,2048]{1,0:T(8,128)(2,1)}) %all-gather.6.cloned.1.call-update) | async-done | bytes 1048592 | tf_op jit(solution)/shard_map/all_gather | solution.py:97
  126.5 6.2 %fusion.5 = (f32[64,4,4]{2,1,0:T(4,128)S(1)}, f32[64,4,4,1024]{3,2,1,0:T(4,128)S(1)}) fusion(pred[64,1024]{1,0:T(8,128)(4,1)} %broadcast_compare_fusion, bf16[64,1024,128]{1,2,0:T(8,128)(2,1)} %bitcast.67, bf16[64,4,4,32]{3,2,1,0:T(4,128)(2,1)S(1)} %get-tuple-element.101, bf16[64,4,4,32]{3,2,1,0:T(4,128)(2,1)S(1)} %get-tuple-element.100), kind=kOutput, calls=%fused_computation.18 | convolution fusion | flops 137624576 | bytes 12783616 | tf_op jit(solution)/shard_map/rjgd,rpd->rjgp/dot_general | solution.py:116
  132.6 3.7 convert_reduce_fusion
  136.4 6.8 %fusion.3 = f32[64,4,4,64]{3,2,1,0:T(4,128)} fusion(bf16[64,4,4,1024]{3,2,1,0:T(4,128)(2,1)S(1)} %get-tuple-element.99, bf16[64,1024,128]{1,2,0:T(8,128)(2,1)} %bitcast.68), kind=kOutput, calls=%fused_computation.12 | convolution fusion | flops 134217728 | bytes 10747904 | tf_op jit(solution)/shard_map/rjgp,rpd->rjgd/dot_general | solution.py:126
  143.3 30.5 %all-gather.1 = f32[1024,4,4]{2,1,0:T(4,128)S(1)} all-gather(f32[64,4,4]{2,1,0:T(4,128)S(1)} %get-tuple-element.98), channel_id=3, replica_groups=mesh['tok'=4,'seq'=16,'kv'=2] {'seq'}, dimensions={0}, use_global_device_ids=true | all-gather | bytes 69632 | tf_op jit(solution)/shard_map/all_gather | solution.py:31
  175.2 31.3 %all-gather = f32[1024,4,4]{2,1,0:T(4,128)S(1)} all-gather(f32[64,4,4]{2,1,0:T(4,128)S(1)} %get-tuple-element.110), channel_id=2, replica_groups=mesh['tok'=4,'seq'=16,'kv'=2] {'seq'}, dimensions={0}, use_global_device_ids=true | all-gather | bytes 69632 | tf_op jit(solution)/shard_map/all_gather | solution.py:31
  208.8 3.3 fusion.39
  214.4 2.6 copy.93
  219.2 7.1 %all-gather.8.cloned.1.call-done = f32[1024,4,4,64]{3,2,1,0:T(4,128)} async-done(((f32[64,4,4,64]{3,2,1,0:T(4,128)}), f32[1024,4,4,64]{3,2,1,0:T(4,128)}) %all-gather.8.cloned.1.call-update) | async-done | bytes 4194320 | tf_op jit(solution)/shard_map/all_gather | solution.py:31
  226.4 7.7 %slice.77 = f32[960,4,4,64]{3,2,1,0:T(4,128)} slice(f32[1024,4,4,64]{3,2,1,0:T(4,128)} %all-gather.8.cloned.1.call-done), slice={[64:1024], [0:4], [0:4], [0:64]} | slice | bytes 7864320 | tf_op jit(solution)/shard_map/slice | solution.py:33
  234.1 53.9 %while.14 = (s32[]{:T(128)}, f32[64,4,4]{0,2,1:T(4,128)S(1)}, f32[64,4,4]{0,2,1:T(4,128)S(1)}, f32[64,4,4,64]{3,2,1,0:T(4,128)S(1)}, f32[15,64,4,4]{1,3,2,0:T(4,...) while((s32[]{:T(128)}, f32[64,4,4]{0,2,1:T(4,128)S(1)}, ...), condition=%wide.region_5.6_spmd, body=%wide.region_4.5_spmd.sunk | while | flops 202754 | bytes 843877 | solution.py:34
  295.2 27.4 %reduce-scatter.3.cloned.1.call-done = f32[32,128]{1,0:T(8,128)} async-done(((f32[256,128]{1,0:T(8,128)}), f32[32,128]{1,0:T(8,128)}) %reduce-scatter.3.cloned.1.call-update) | async-done | bytes 16400 | tf_op jit(solution)/shard_map/reduce_scatter | solution.py:157
  324.9 5.5 %collective-permute-done = bf16[32,128]{1,0:T(8,128)(2,1)S(1)} collective-permute-done((bf16[32,128]{1,0:T(8,128)(2,1)S(1)}, bf16[32,128]{1,0:T(8,128)(2,1)S(1)}, u32[]{:S(2)}, u32[]{:S(2)}) %collective-permute-start) | collective-permute-done | bytes 8224 | tf_op jit(solution)/shard_map/ppermute | solution.py:19
  330.3 5.3 %collective-permute-start.8 = (bf16[32,128]{1,0:T(8,128)(2,1)S(1)}, bf16[32,128]{1,0:T(8,128)(2,1)S(1)}, u32[]{:S(2)}, u32[]{:S(2)}) collective-permute-start(bf16[32,128]{1,0:T(8,128)(2,1)S(1)} %fusion.32), channel_id=1, source_target_pairs={{0,30},{2,0},{4,2},{6,4},{8,6},{10,8},{12,10},{14,12},{16,14},{18,... | collective-permute-start | bytes 24584 | tf_op jit(solution)/shard_map/ppermute | solution.py:22
  337.3 5.3 %collective-permute-start.9 = (bf16[32,128]{1,0:T(8,128)(2,1)S(1)}, bf16[32,128]{1,0:T(8,128)(2,1)S(1)}, u32[]{:S(2)}, u32[]{:S(2)}) collective-permute-start(bf16[32,128]{1,0:T(8,128)(2,1)S(1)} %collective-permute-done.8), channel_id=1, source_target_pairs={{0,30},{2,0},{4,2},{6,4},{8,6},{10,8},{12,10},{14,12},{16,14},{18,... | collective-permute-start | bytes 24584 | tf_op jit(solution)/shard_map/ppermute | solution.py:22
  344.3 5.3 %collective-permute-start.10 = (bf16[32,128]{1,0:T(8,128)(2,1)S(1)}, bf16[32,128]{1,0:T(8,128)(2,1)S(1)}, u32[]{:S(2)}, u32[]{:S(2)}) collective-permute-start(bf16[32,128]{1,0:T(8,128)(2,1)S(1)} %collective-permute-done.9), channel_id=1, source_target_pairs={{0,30},{2,0},{4,2},{6,4},{8,6},{10,8},{12,10},{14,12},{16,14},{18,... | collective-permute-start | bytes 24584 | tf_op jit(solution)/shard_map/ppermute | solution.py:22
  351.2 5.3 %collective-permute-start.11 = (bf16[32,128]{1,0:T(8,128)(2,1)S(1)}, bf16[32,128]{1,0:T(8,128)(2,1)S(1)}, u32[]{:S(2)}, u32[]{:S(2)}) collective-permute-start(bf16[32,128]{1,0:T(8,128)(2,1)S(1)} %collective-permute-done.10), channel_id=1, source_target_pairs={{0,30},{2,0},{4,2},{6,4},{8,6},{10,8},{12,10},{14,12},{16,14},{18,... | collective-permute-start | bytes 24584 | tf_op jit(solution)/shard_map/ppermute | solution.py:22
  358.2 5.3 %collective-permute-start.12 = (bf16[32,128]{1,0:T(8,128)(2,1)S(1)}, bf16[32,128]{1,0:T(8,128)(2,1)S(1)}, u32[]{:S(2)}, u32[]{:S(2)}) collective-permute-start(bf16[32,128]{1,0:T(8,128)(2,1)S(1)} %collective-permute-done.11), channel_id=1, source_target_pairs={{0,30},{2,0},{4,2},{6,4},{8,6},{10,8},{12,10},{14,12},{16,14},{18,... | collective-permute-start | bytes 24584 | tf_op jit(solution)/shard_map/ppermute | solution.py:22
  365.2 5.3 %collective-permute-start.13 = (bf16[32,128]{1,0:T(8,128)(2,1)S(1)}, bf16[32,128]{1,0:T(8,128)(2,1)S(1)}, u32[]{:S(2)}, u32[]{:S(2)}) collective-permute-start(bf16[32,128]{1,0:T(8,128)(2,1)S(1)} %collective-permute-done.12), channel_id=1, source_target_pairs={{0,30},{2,0},{4,2},{6,4},{8,6},{10,8},{12,10},{14,12},{16,14},{18,... | collective-permute-start | bytes 24584 | tf_op jit(solution)/shard_map/ppermute | solution.py:22
  372.2 5.4 %collective-permute-start.14 = (bf16[32,128]{1,0:T(8,128)(2,1)S(1)}, bf16[32,128]{1,0:T(8,128)(2,1)S(1)}, u32[]{:S(2)}, u32[]{:S(2)}) collective-permute-start(bf16[32,128]{1,0:T(8,128)(2,1)S(1)} %collective-permute-done.13), channel_id=1, source_target_pairs={{0,30},{2,0},{4,2},{6,4},{8,6},{10,8},{12,10},{14,12},{16,14},{18,... | collective-permute-start | bytes 24584 | tf_op jit(solution)/shard_map/ppermute | solution.py:22
  381.7 3.2 fusion.13
  384.9 70.8 %reduce-scatter.5.cloned.1.call-done = f32[32,128]{1,0:T(8,128)} async-done(((f32[32,2048]{1,0:T(8,128)}), f32[32,128]{1,0:T(8,128)}) %reduce-scatter.5.cloned.1.call-update) | async-done | bytes 16400 | tf_op jit(solution)/shard_map/reduce_scatter | solution.py:177
  (208 shorter events, 101.5 us)
Async XLA Ops:
  6.5 375.2 %copy-start = (bf16[512,2048]{1,0:T(8,128)(2,1)S(1)}, bf16[512,2048]{1,0:T(8,128)(2,1)}, u32[]{:S(2)}) copy-start(bf16[512,2048]{1,0:T(8,128)(2,1)} %param.27) | copy-start | bytes 6291460
  6.5 67.6 %all-reduce.2.cloned.1.call-start = ((), (), s32[]{:S(2)}) async-start(), calls=%async_computation.2 | async-start | bytes 131072 | tf_op jit(solution)/shard_map/psum | solution.py:95
  12.8 106.1 %all-gather.6.cloned.1.call-start = ((), (), s32[]{:S(2)}) async-start(), calls=%async_computation.3 | async-start | bytes 1114112 | tf_op jit(solution)/shard_map/all_gather | solution.py:97
  74.1 152.2 %all-gather.8.cloned.1.call-start = ((), (), s32[]{:S(2)}) async-start(), calls=%async_computation.6 | async-start | bytes 8912896 | tf_op jit(solution)/shard_map/all_gather | solution.py:31
  143.2 179.4 %reduce-scatter.3.cloned.1.call-start = ((), (), s32[]{:S(2)}) async-start(), calls=%async_computation.4 | async-start | bytes 147456 | tf_op jit(solution)/shard_map/reduce_scatter | solution.py:157
  143.3 69.2 %copy-start.8 = (pred[4,4]{1,0:T(4,128)(4,1)}, pred[4,4]{1,0:T(4,128)(4,1)S(1)}, u32[]{:S(2)}) copy-start(pred[4,4]{1,0:T(4,128)(4,1)S(1)} %iota_compare_fusion) | copy-start | bytes 52
  234.1 55.6 %copy-start.2 = (bf16[64,4,4,4]{3,2,1,0:T(4,128)(2,1)S(1)}, bf16[64,4,4,4]{3,2,1,0:T(4,128)(2,1)}, u32[]{:S(2)}) copy-start(bf16[64,4,4,4]{3,2,1,0:T(4,128)(2,1)} %copy.102) | copy-start | bytes 24580
  289.7 82.4 %copy-start.6 = (bf16[2048]{0:T(1024)(128)(2,1)S(1)}, bf16[2048]{0:T(1024)(128)(2,1)}, u32[]{:S(2)}) copy-start(bf16[2048]{0:T(1024)(128)(2,1)} %param.24) | copy-start | bytes 12292
  293.6 162.1 %reduce-scatter.5.cloned.1.call-start = ((), (), s32[]{:S(2)}) async-start(), calls=%async_computation.5 | async-start | bytes 278528 | tf_op jit(solution)/shard_map/reduce_scatter | solution.py:177
  323.3 7.0 %collective-permute-start = (bf16[32,128]{1,0:T(8,128)(2,1)S(1)}, bf16[32,128]{1,0:T(8,128)(2,1)S(1)}, u32[]{:S(2)}, u32[]{:S(2)}) collective-permute-start(bf16[32,128]{1,0:T(8,128)(2,1)S(1)} %fusion.32), channel_id=1, source_target_pairs={{0,2},{2,4},{4,6},{6,8},{8,10},{10,12},{12,14},{14,16},{16,18},{18... | collective-permute-start | bytes 24584 | tf_op jit(solution)/shard_map/ppermute | solution.py:19
  330.3 7.0 %collective-permute-start.1 = (bf16[32,128]{1,0:T(8,128)(2,1)S(1)}, bf16[32,128]{1,0:T(8,128)(2,1)S(1)}, u32[]{:S(2)}, u32[]{:S(2)}) collective-permute-start(bf16[32,128]{1,0:T(8,128)(2,1)S(1)} %collective-permute-done), channel_id=1, source_target_pairs={{0,2},{2,4},{4,6},{6,8},{8,10},{10,12},{12,14},{14,16},{16,18},{18... | collective-permute-start | bytes 24584 | tf_op jit(solution)/shard_map/ppermute | solution.py:19
  330.3 7.0 %collective-permute-start.8 = (bf16[32,128]{1,0:T(8,128)(2,1)S(1)}, bf16[32,128]{1,0:T(8,128)(2,1)S(1)}, u32[]{:S(2)}, u32[]{:S(2)}) collective-permute-start(bf16[32,128]{1,0:T(8,128)(2,1)S(1)} %fusion.32), channel_id=1, source_target_pairs={{0,30},{2,0},{4,2},{6,4},{8,6},{10,8},{12,10},{14,12},{16,14},{18,... | collective-permute-start | bytes 24584 | tf_op jit(solution)/shard_map/ppermute | solution.py:22
  337.3 7.0 %collective-permute-start.2 = (bf16[32,128]{1,0:T(8,128)(2,1)S(1)}, bf16[32,128]{1,0:T(8,128)(2,1)S(1)}, u32[]{:S(2)}, u32[]{:S(2)}) collective-permute-start(bf16[32,128]{1,0:T(8,128)(2,1)S(1)} %collective-permute-done.1), channel_id=1, source_target_pairs={{0,2},{2,4},{4,6},{6,8},{8,10},{10,12},{12,14},{14,16},{16,18},{18... | collective-permute-start | bytes 24584 | tf_op jit(solution)/shard_map/ppermute | solution.py:19
  337.3 7.0 %collective-permute-start.9 = (bf16[32,128]{1,0:T(8,128)(2,1)S(1)}, bf16[32,128]{1,0:T(8,128)(2,1)S(1)}, u32[]{:S(2)}, u32[]{:S(2)}) collective-permute-start(bf16[32,128]{1,0:T(8,128)(2,1)S(1)} %collective-permute-done.8), channel_id=1, source_target_pairs={{0,30},{2,0},{4,2},{6,4},{8,6},{10,8},{12,10},{14,12},{16,14},{18,... | collective-permute-start | bytes 24584 | tf_op jit(solution)/shard_map/ppermute | solution.py:22
  344.3 7.0 %collective-permute-start.3 = (bf16[32,128]{1,0:T(8,128)(2,1)S(1)}, bf16[32,128]{1,0:T(8,128)(2,1)S(1)}, u32[]{:S(2)}, u32[]{:S(2)}) collective-permute-start(bf16[32,128]{1,0:T(8,128)(2,1)S(1)} %collective-permute-done.2), channel_id=1, source_target_pairs={{0,2},{2,4},{4,6},{6,8},{8,10},{10,12},{12,14},{14,16},{16,18},{18... | collective-permute-start | bytes 24584 | tf_op jit(solution)/shard_map/ppermute | solution.py:19
  344.3 7.0 %collective-permute-start.10 = (bf16[32,128]{1,0:T(8,128)(2,1)S(1)}, bf16[32,128]{1,0:T(8,128)(2,1)S(1)}, u32[]{:S(2)}, u32[]{:S(2)}) collective-permute-start(bf16[32,128]{1,0:T(8,128)(2,1)S(1)} %collective-permute-done.9), channel_id=1, source_target_pairs={{0,30},{2,0},{4,2},{6,4},{8,6},{10,8},{12,10},{14,12},{16,14},{18,... | collective-permute-start | bytes 24584 | tf_op jit(solution)/shard_map/ppermute | solution.py:22
  351.2 7.0 %collective-permute-start.4 = (bf16[32,128]{1,0:T(8,128)(2,1)S(1)}, bf16[32,128]{1,0:T(8,128)(2,1)S(1)}, u32[]{:S(2)}, u32[]{:S(2)}) collective-permute-start(bf16[32,128]{1,0:T(8,128)(2,1)S(1)} %collective-permute-done.3), channel_id=1, source_target_pairs={{0,2},{2,4},{4,6},{6,8},{8,10},{10,12},{12,14},{14,16},{16,18},{18... | collective-permute-start | bytes 24584 | tf_op jit(solution)/shard_map/ppermute | solution.py:19
  351.2 7.0 %collective-permute-start.11 = (bf16[32,128]{1,0:T(8,128)(2,1)S(1)}, bf16[32,128]{1,0:T(8,128)(2,1)S(1)}, u32[]{:S(2)}, u32[]{:S(2)}) collective-permute-start(bf16[32,128]{1,0:T(8,128)(2,1)S(1)} %collective-permute-done.10), channel_id=1, source_target_pairs={{0,30},{2,0},{4,2},{6,4},{8,6},{10,8},{12,10},{14,12},{16,14},{18,... | collective-permute-start | bytes 24584 | tf_op jit(solution)/shard_map/ppermute | solution.py:22
  358.2 7.0 %collective-permute-start.5 = (bf16[32,128]{1,0:T(8,128)(2,1)S(1)}, bf16[32,128]{1,0:T(8,128)(2,1)S(1)}, u32[]{:S(2)}, u32[]{:S(2)}) collective-permute-start(bf16[32,128]{1,0:T(8,128)(2,1)S(1)} %collective-permute-done.4), channel_id=1, source_target_pairs={{0,2},{2,4},{4,6},{6,8},{8,10},{10,12},{12,14},{14,16},{16,18},{18... | collective-permute-start | bytes 24584 | tf_op jit(solution)/shard_map/ppermute | solution.py:19
  358.2 7.0 %collective-permute-start.12 = (bf16[32,128]{1,0:T(8,128)(2,1)S(1)}, bf16[32,128]{1,0:T(8,128)(2,1)S(1)}, u32[]{:S(2)}, u32[]{:S(2)}) collective-permute-start(bf16[32,128]{1,0:T(8,128)(2,1)S(1)} %collective-permute-done.11), channel_id=1, source_target_pairs={{0,30},{2,0},{4,2},{6,4},{8,6},{10,8},{12,10},{14,12},{16,14},{18,... | collective-permute-start | bytes 24584 | tf_op jit(solution)/shard_map/ppermute | solution.py:22
  365.2 7.0 %collective-permute-start.6 = (bf16[32,128]{1,0:T(8,128)(2,1)S(1)}, bf16[32,128]{1,0:T(8,128)(2,1)S(1)}, u32[]{:S(2)}, u32[]{:S(2)}) collective-permute-start(bf16[32,128]{1,0:T(8,128)(2,1)S(1)} %collective-permute-done.5), channel_id=1, source_target_pairs={{0,2},{2,4},{4,6},{6,8},{8,10},{10,12},{12,14},{14,16},{16,18},{18... | collective-permute-start | bytes 24584 | tf_op jit(solution)/shard_map/ppermute | solution.py:19
  365.2 7.0 %collective-permute-start.13 = (bf16[32,128]{1,0:T(8,128)(2,1)S(1)}, bf16[32,128]{1,0:T(8,128)(2,1)S(1)}, u32[]{:S(2)}, u32[]{:S(2)}) collective-permute-start(bf16[32,128]{1,0:T(8,128)(2,1)S(1)} %collective-permute-done.12), channel_id=1, source_target_pairs={{0,30},{2,0},{4,2},{6,4},{8,6},{10,8},{12,10},{14,12},{16,14},{18,... | collective-permute-start | bytes 24584 | tf_op jit(solution)/shard_map/ppermute | solution.py:22
  372.1 7.0 %collective-permute-start.7 = (bf16[32,128]{1,0:T(8,128)(2,1)S(1)}, bf16[32,128]{1,0:T(8,128)(2,1)S(1)}, u32[]{:S(2)}, u32[]{:S(2)}) collective-permute-start(bf16[32,128]{1,0:T(8,128)(2,1)S(1)} %collective-permute-done.6), channel_id=1, source_target_pairs={{0,2},{2,4},{4,6},{6,8},{8,10},{10,12},{12,14},{14,16},{16,18},{18... | collective-permute-start | bytes 24584 | tf_op jit(solution)/shard_map/ppermute | solution.py:19
  372.2 7.1 %collective-permute-start.14 = (bf16[32,128]{1,0:T(8,128)(2,1)S(1)}, bf16[32,128]{1,0:T(8,128)(2,1)S(1)}, u32[]{:S(2)}, u32[]{:S(2)}) collective-permute-start(bf16[32,128]{1,0:T(8,128)(2,1)S(1)} %collective-permute-done.13), channel_id=1, source_target_pairs={{0,30},{2,0},{4,2},{6,4},{8,6},{10,8},{12,10},{14,12},{16,14},{18,... | collective-permute-start | bytes 24584 | tf_op jit(solution)/shard_map/ppermute | solution.py:22
  (7 other events, 109.0 us)
Sparse Core Ops, SparseCore 0:
  12.9 61.1 all-reduce.1
  76.4 42.4 all-gather.5
  143.4 82.9 all-gather.7
  293.7 28.8 reduce-scatter.2
  385.1 70.6 reduce-scatter.4
